TPU v7x, 32 devices: a whole 2x2x4 slice. The times are simulated.
32 devices in a mesh: wide: 2 (over x), grow: 4 (over y, core), gcol: 4 (over z).
Axes of the slice: x: 2, y: 2, z: 4, core: 2. Of those that a mesh axis runs over, the one named last changes fastest.
Arguments:
- diag_block: float32 [2, 1024, 1024], P('wide', ('grow', 'gcol')), as said below
- lower_block: float32 [2, 3072, 1024], P('wide', ('grow', 'gcol')), may hold values from -0.1875 to 0.1875
- trailing_block: float32 [2, 3072, 3072], P('wide', 'grow', 'gcol'), as said below
- parent_front: float32 [4, 2048, 8192], P('grow', 'wide', 'gcol'), may hold values from -3 to 3
- row_map: int32 [2, 24], replicated, may hold values from 0 to 63, as said below
Outputs:
- factor: float32 [2, 1024, 1024], P('wide', ('grow', 'gcol'))
- panel: float32 [2, 3072, 1024], P('wide', ('grow', 'gcol'))
- parent: float32 [4, 2048, 8192], P('grow', 'wide', 'gcol')
Inputs may be any that keep to these rules, and one draw needn't show every extreme that they name: Each diag_block[g] is symmetric and positive definite. Each trailing_block[g] is symmetric. `row_map`: the blocks of one child are distinct, and child block b goes to a grandparent block p with p // 16 equal to b // 6.
All inputs are finite; a program needn't handle non-finite values.
Results may differ from a plain program's by a relative error of at most 0.0003.
Values sent between devices are 32-bit elements; how exact they have to be, the bound alone decides.
A program may use at most 128 MiB of HBM per device.

v0:
```python
import jax
import jax.numpy as jnp
from jax import lax
from jax.sharding import PartitionSpec as P

BLOCK = 128


def ranked(local, per_owner, count):
    target = local // per_owner
    same = target[..., :, None] == target[..., None, :]
    earlier = jnp.arange(count)[None, :] < jnp.arange(count)[:, None]
    return (target, jnp.sum((same & earlier).astype(jnp.int32), axis=-1))


def body(diag_block, lower_block, trailing_block, parent_front, row_map):
    highest = lax.Precision.HIGHEST
    whole = lax.all_gather(diag_block[0], ("grow", "gcol"), axis=0, tiled=True)
    factor = jnp.linalg.cholesky(whole)
    share = diag_block.shape[1]
    factor_rows = lax.dynamic_slice_in_dim(
        factor, lax.axis_index(("grow", "gcol")) * share, share, 0
    )
    panel = jax.scipy.linalg.solve_triangular(factor, lower_block[0].T, lower=True).T
    row_part = lax.all_gather(panel, "gcol", axis=0, tiled=True)
    column_index = lax.axis_index("gcol")
    every = lax.all_gather(row_part, "grow", axis=0, tiled=True)
    col_part = lax.dynamic_slice_in_dim(
        every, column_index * row_part.shape[0], row_part.shape[0], 0
    )
    update = lax.dot_general(
        row_part,
        col_part,
        (((1,), (1,)), ((), ())),
        precision=highest,
        preferred_element_type=jnp.float32,
    )
    schur = trailing_block[0] - update
    owners = lax.axis_size("wide")
    child = lax.axis_index("wide")
    row_index = lax.axis_index("grow")
    width_blocks = schur.shape[0] // BLOCK
    quarter_blocks = parent_front.shape[1] * owners // BLOCK
    column_blocks = parent_front.shape[2] // BLOCK
    row_local = (
        lax.dynamic_slice_in_dim(row_map, row_index * width_blocks, width_blocks, 1)
        % quarter_blocks
    )
    col_local = (
        lax.dynamic_slice_in_dim(row_map, column_index * width_blocks, width_blocks, 1)
        % column_blocks
    )
    grid = jnp.arange(column_blocks, dtype=jnp.int32)
    per_owner = quarter_blocks // owners
    slots = min(width_blocks, per_owner)
    mine_rows = lax.dynamic_slice_in_dim(row_local, child, 1, 0)[0]
    target, rank = ranked(mine_rows, per_owner, width_blocks)
    slot_of = target * slots + rank
    send_place = (slot_of[None, :] == jnp.arange(owners * slots, dtype=jnp.int32)[:, None]).astype(
        jnp.float32
    )
    outgoing = jnp.einsum(
        "sb,bxy->sxy",
        send_place,
        schur.reshape(width_blocks, BLOCK, schur.shape[1]),
        precision=highest,
    )
    incoming = lax.all_to_all(outgoing, "wide", split_axis=0, concat_axis=0, tiled=True)
    source_target, source_rank = ranked(row_local, per_owner, width_blocks)
    offset = row_local - child * per_owner
    chosen = (source_target == child)[:, :, None, None]
    by_slot = (
        source_rank[:, :, None, None] == jnp.arange(slots, dtype=jnp.int32)[None, None, :, None]
    )
    by_block = (
        offset[:, :, None, None] == jnp.arange(per_owner, dtype=jnp.int32)[None, None, None, :]
    )
    landing = jnp.sum((chosen & by_slot & by_block).astype(jnp.float32), axis=1)
    arrived = incoming.reshape(owners, slots, BLOCK, width_blocks, BLOCK)
    sectioned = jnp.einsum("gsp,gsxcy->gpxcy", landing, arrived, precision=highest)
    col_place = (col_local[:, None, :] == grid[None, :, None]).astype(jnp.float32)
    spread = jnp.einsum("gpxcy,gqc->pxqy", sectioned, col_place, precision=highest)
    summed = spread.reshape(per_owner * BLOCK, column_blocks * BLOCK)
    parent = parent_front + summed[None]
    return (factor_rows[None], panel[None], parent)


def solution(mesh):
    placed = (
        P("wide", ("grow", "gcol"), None),
        P("wide", ("grow", "gcol"), None),
        P("wide", "grow", "gcol"),
        P("grow", "wide", "gcol"),
        P(),
    )
    return jax.shard_map(
        body,
        mesh=mesh,
        in_specs=placed,
        out_specs=(
            P("wide", ("grow", "gcol"), None),
            P("wide", ("grow", "gcol"), None),
            P("grow", "wide", "gcol"),
        ),
        check_vma=False,
    )
```

profile of v0, /device:TPU:0, one launch (start us, length us, event | category | flops | bytes accessed | tf_op | source)
XLA Modules:
  0.0 688.5 jit_solution(11161298639368226633)
XLA Ops:
  9.2 54.6 %all-gather.9.cloned.1.call-done = f32[1,1024,1024]{2,0,1:T(1,128)} async-done(((f32[1,64,1024]{2,0,1:T(1,128)}), f32[1,1024,1024]{2,0,1:T(1,128)}) %all-gather.9.cloned.1.call-update) | async-done | bytes 4194320 | tf_op jit(solution)/shard_map/all_gather | solution.py:18
  63.9 10.9 %copy.24 = f32[1,1024,1024]{1,2,0:T(8,128)} copy(f32[1,1024,1024]{2,0,1:T(1,128)} %all-gather.9.cloned.1.call-done) | data formatting | bytes 8388608 | tf_op jit(solution)/shard_map/all_gather | solution.py:18
  81.7 11.7 %cholesky.223 = f32[128,128]{1,0:T(8,128)S(1)} custom-call(f32[128,128]{1,0:T(8,128)S(1)} %cholesky.580), custom_call_target="Cholesky" | custom-call | tf_op jit(solution)/shard_map/jit(cholesky)/cholesky | solution.py:19
  96.0 9.8 %custom-call.63 = f32[1,128,128]{1,2,0:T(8,128)S(1)} custom-call(f32[1,128,128]{2,1,0:T(8,128)S(1)} %get-tuple-element.72), custom_call_target="InvertDiagBlocksLowerTriangular" | custom-call | tf_op jit(solution)/shard_map/jit(cholesky)/cholesky | solution.py:19
  109.7 11.8 %cholesky.244 = f32[128,128]{1,0:T(8,128)S(1)} custom-call(f32[128,128]{1,0:T(8,128)S(1)} %cholesky.584), custom_call_target="Cholesky" | custom-call | tf_op jit(solution)/shard_map/jit(cholesky)/cholesky | solution.py:19
  122.2 9.8 %custom-call.64 = f32[1,128,128]{1,2,0:T(8,128)S(1)} custom-call(f32[1,128,128]{2,1,0:T(8,128)S(1)} %get-tuple-element.69), custom_call_target="InvertDiagBlocksLowerTriangular" | custom-call | tf_op jit(solution)/shard_map/jit(cholesky)/cholesky | solution.py:19
  135.3 11.7 %cholesky.468 = f32[128,128]{1,0:T(8,128)S(1)} custom-call(f32[128,128]{1,0:T(8,128)S(1)} %cholesky.589), custom_call_target="Cholesky" | custom-call | tf_op jit(solution)/shard_map/jit(cholesky)/cholesky | solution.py:19
  147.7 9.8 %custom-call.65 = f32[1,128,128]{1,2,0:T(8,128)S(1)} custom-call(f32[1,128,128]{2,1,0:T(8,128)S(1)} %get-tuple-element.66), custom_call_target="InvertDiagBlocksLowerTriangular" | custom-call | tf_op jit(solution)/shard_map/jit(cholesky)/cholesky | solution.py:19
  161.0 11.9 %cholesky.487 = f32[128,128]{1,0:T(8,128)S(1)} custom-call(f32[128,128]{1,0:T(8,128)S(1)} %cholesky.594), custom_call_target="Cholesky" | custom-call | tf_op jit(solution)/shard_map/jit(cholesky)/cholesky | solution.py:19
  173.5 9.8 %custom-call.66 = f32[1,128,128]{1,2,0:T(8,128)S(1)} custom-call(f32[1,128,128]{2,1,0:T(8,128)S(1)} %get-tuple-element.63), custom_call_target="InvertDiagBlocksLowerTriangular" | custom-call | tf_op jit(solution)/shard_map/jit(cholesky)/cholesky | solution.py:19
  186.8 11.7 %cholesky.506 = f32[128,128]{1,0:T(8,128)S(1)} custom-call(f32[128,128]{1,0:T(8,128)S(1)} %cholesky.599), custom_call_target="Cholesky" | custom-call | tf_op jit(solution)/shard_map/jit(cholesky)/cholesky | solution.py:19
  199.1 10.2 %custom-call.67 = f32[1,128,128]{1,2,0:T(8,128)S(1)} custom-call(f32[1,128,128]{2,1,0:T(8,128)S(1)} %get-tuple-element.60), custom_call_target="InvertDiagBlocksLowerTriangular" | custom-call | tf_op jit(solution)/shard_map/jit(cholesky)/cholesky | solution.py:19
  212.7 11.7 %cholesky.526 = f32[128,128]{1,0:T(8,128)S(1)} custom-call(f32[128,128]{1,0:T(8,128)S(1)} %cholesky.604), custom_call_target="Cholesky" | custom-call | tf_op jit(solution)/shard_map/jit(cholesky)/cholesky | solution.py:19
  225.0 9.8 %custom-call.68 = f32[1,128,128]{1,2,0:T(8,128)S(1)} custom-call(f32[1,128,128]{2,1,0:T(8,128)S(1)} %get-tuple-element.57), custom_call_target="InvertDiagBlocksLowerTriangular" | custom-call | tf_op jit(solution)/shard_map/jit(cholesky)/cholesky | solution.py:19
  237.8 11.9 %cholesky.546 = f32[128,128]{1,0:T(8,128)S(1)} custom-call(f32[128,128]{1,0:T(8,128)S(1)} %cholesky.609), custom_call_target="Cholesky" | custom-call | tf_op jit(solution)/shard_map/jit(cholesky)/cholesky | solution.py:19
  250.3 9.8 %custom-call.69 = f32[1,128,128]{1,2,0:T(8,128)S(1)} custom-call(f32[1,128,128]{2,1,0:T(8,128)S(1)} %get-tuple-element.54), custom_call_target="InvertDiagBlocksLowerTriangular" | custom-call | tf_op jit(solution)/shard_map/jit(cholesky)/cholesky | solution.py:19
  262.8 11.7 %cholesky.564 = f32[128,128]{1,0:T(8,128)S(1)} custom-call(f32[128,128]{1,0:T(8,128)S(1)} %convolution_subtract_fusion.13), custom_call_target="Cholesky" | custom-call | tf_op jit(solution)/shard_map/jit(cholesky)/cholesky | solution.py:19
  291.7 23.2 %while.1 = (s32[]{:T(128)}, f32[1024,1024]{1,0:T(8,128)}, s32[8,2]{0,1:T(2,128)S(1)}, f32[8,128,128]{2,1,0:T(8,128)S(1)}, s32[]{:T(128)}) while((s32[]{:T(128)}, f32[1024,1024]{1,0:T(8,128)}, s32[8,2]{0,1:T(2,128)S(1)}, f32[8,128,128]{2,1,0:T(8,128)S(1)}, s32[]{:T(128)}) %tuple.64), condition=%wide.while_cond, body=%wide.while_body.sunk | while | flops 2 | bytes 131189 | solution.py:24
  314.9 78.6 %custom-call.70 = f32[8,128,128]{1,2,0:T(8,128)S(1)} custom-call(f32[8,128,128]{2,1,0:T(8,128)S(1)} %get-tuple-element.10), custom_call_target="InvertDiagBlocksLowerTriangular" | custom-call | tf_op jit(solution)/shard_map/jit(_solve_triangular)/triangular_solve | solution.py:24
  407.0 61.7 %all-gather.5.cloned.1.call-done = f32[768,1024]{1,0:T(8,128)} async-done(((f32[192,1024]{1,0:T(8,128)}), f32[768,1024]{1,0:T(8,128)}) %all-gather.5.cloned.1.call-update) | async-done | bytes 3145744 | tf_op jit(solution)/shard_map/all_gather | solution.py:25
  469.0 81.9 %all-gather.7.cloned.1.call-done = f32[3072,1024]{1,0:T(8,128)} async-done(((f32[768,1024]{1,0:T(8,128)}), f32[3072,1024]{1,0:T(8,128)}) %all-gather.7.cloned.1.call-update) | async-done | bytes 12582928 | tf_op jit(solution)/shard_map/all_gather | solution.py:27
  551.0 10.5 %bitcast_subtract_fusion = f32[768,768]{1,0:T(8,128)S(1)} fusion(f32[1,768,768]{2,1,0:T(8,128)} %param.7, f32[768,1024]{1,0:T(8,128)S(1)} %copy-done, f32[3072,1024]{1,0:T(8,128)} %all-gather.7.cloned.1.call-done, s32[]{:T(128)S(6)} %select_n.58), kind=kOutput, calls=%fused_computation.14 | convolution fusion | flops 7248347136 | bytes 11010052 | tf_op jit(solution)/shard_map/dot_general | solution.py:31
  579.1 51.2 %all-to-all-done = f32[12,128,768]{2,1,0:T(8,128)} async-done(((f32[12,128,768]{2,1,0:T(8,128)}), f32[12,128,768]{2,1,0:T(8,128)}, u32[]{:S(2)}, u32[]{:S(2)}) %all-to-all-start) | async-done | bytes 4718624 | tf_op jit(solution)/shard_map/all_to_all | solution.py:68
  669.9 11.9 %add.130 = f32[1,1024,2048]{2,1,0:T(8,128)} add(f32[1,1024,2048]{2,1,0:T(8,128)} %param.8, f32[1,1024,2048]{2,1,0:T(8,128)} %broadcast_in_dim_reshape.3) | non-fusion elementwise | flops 2097152 | bytes 25165824 | tf_op jit(solution)/shard_map/add | solution.py:84
  (122 shorter events, 144.4 us)
Async XLA Ops:
  7.2 56.7 %all-gather.9.cloned.1.call-start = ((), (), s32[]{:S(2)}) async-start(), calls=%async_computation.3 | async-start | bytes 4456448 | tf_op jit(solution)/shard_map/all_gather | solution.py:18
  9.2 459.5 %all-gather.5.cloned.1.call-start = ((), (), s32[]{:S(2)}) async-start(), calls=%async_computation.1 | async-start | bytes 3932160 | tf_op jit(solution)/shard_map/all_gather | solution.py:25
  79.8 1.9 copy-start.1
  284.8 108.7 %copy-start.3 = (f32[1,192,1024]{2,1,0:T(8,128)S(1)}, f32[1,192,1024]{2,1,0:T(8,128)}, u32[]{:S(2)}) copy-start(f32[1,192,1024]{2,1,0:T(8,128)} %param.6) | copy-start | bytes 2359300
  399.9 68.8 %copy-start.4 = (s32[2,24]{1,0:T(2,128)S(1)}, s32[2,24]{1,0:T(2,128)}, u32[]{:S(2)}) copy-start(s32[2,24]{1,0:T(2,128)} %param.9) | copy-start | bytes 580
  405.6 0.9 copy-start.2
  406.5 144.4 %all-gather.7.cloned.1.call-start = ((), (), s32[]{:S(2)}) async-start(), calls=%async_computation.2 | async-start | bytes 15728640 | tf_op jit(solution)/shard_map/all_gather | solution.py:27
  468.6 82.3 %copy-start = (f32[768,1024]{1,0:T(8,128)S(1)}, f32[768,1024]{1,0:T(8,128)}, u32[]{:S(2)}) copy-start(f32[768,1024]{1,0:T(8,128)} %all-gather.5.cloned.1.call-done) | copy-start | bytes 9437188
  570.8 59.5 %all-to-all-start = ((f32[12,128,768]{2,1,0:T(8,128)}), f32[12,128,768]{2,1,0:T(8,128)}, u32[]{:S(2)}, u32[]{:S(2)}) async-start(f32[12,128,768]{2,1,0:T(8,128)} %copy.30), calls=%async_computation | async-start | bytes 9437184 | tf_op jit(solution)/shard_map/all_to_all | solution.py:68
Sparse Core Ops, SparseCore 0:
  10.8 53.0 all-gather.8
  406.6 61.9 all-gather.4
  470.2 80.7 all-gather.6
where the time goes:
time: 699 us; the launch traced here: 688 us
  other arithmetic  276 us (39%)
  waiting for transfers between devices  249 us (36%)
  local copies, waits for them, and re-layouts  69.7 us (10%)
  matrix products  67.8 us (10%)
  between operations  19.4 us (3%)
    another operation x30, other arithmetic, body(): factor = jnp.linalg.cholesky(whole)  172 us
    another operation x3, other arithmetic, body(): jax.scipy.linalg.solve_triangular(factor, lower_block[0].T, lower=True)  85.5 us
    all_gather x1, waiting for transfers between devices, body(): every = lax.all_gather(row_part, 'grow', axis=0, tiled=True)  81.9 us
    all_gather x1, waiting for transfers between devices, body(): row_part = lax.all_gather(panel, 'gcol', axis=0, tiled=True)  61.7 us
    all_gather x1, waiting for transfers between devices, body(): whole = lax.all_gather(diag_block[0], ('grow', 'gcol'), axis=0, tiled=True)  54.6 us
    all_to_all x1, waiting for transfers between devices, body(): lax.all_to_all(outgoing, 'wide', split_axis=0, concat_axis=0, tiled=True)  51.2 us
    another operation x24, local copies, waits for them, and re-layouts  23 us
    another operation x14, matrix products, body(): factor = jnp.linalg.cholesky(whole)  22.9 us
  transfers between devices with their start and end apart: 4, of which 4 were waited for; matrix products, arithmetic and copies ran while one was open for 0% of the time, Pallas kernels for 0%

commit v1 on v0

v1 whole, which is shorter than its diff:
```python
import functools

import jax
import jax.numpy as jnp
from jax import lax
from jax.experimental import pallas as pl
from jax.experimental.pallas import tpu as pltpu
from jax.sharding import PartitionSpec as P

BLOCK = 128
HALF = 64
F32 = jnp.float32
BF16 = jnp.bfloat16
NT = (((1,), (1,)), ((), ()))
NN = (((1,), (0,)), ((), ()))
VMEM = pl.BlockSpec(memory_space=pltpu.VMEM)
SMEM = pl.BlockSpec(memory_space=pltpu.SMEM)


def full_dot(a, b, dims):
    return lax.dot_general(
        a, b, dims, precision=lax.Precision.HIGHEST, preferred_element_type=F32
    )


def parts(x):
    high = x.astype(BF16)
    return high, (x - high.astype(F32)).astype(BF16)


def split_dot(a, b, dims):
    one = functools.partial(lax.dot_general, dimension_numbers=dims, preferred_element_type=F32)
    return one(a[0], b[0]) + (one(a[0], b[1]) + one(a[1], b[0]))


def factor_half(block):
    half = block.shape[0]
    rows = lax.broadcasted_iota(jnp.int32, (half, half), 0)
    cols = lax.broadcasted_iota(jnp.int32, (half, half), 1)
    eye = jnp.where(rows == cols, 1.0, 0.0).astype(F32)
    full = jnp.concatenate([block, eye], axis=1)
    count = half // 8
    wide = (8, 2 * half)
    groups = [full[8 * s : 8 * s + 8] for s in range(count)]
    sub = lax.broadcasted_iota(jnp.int32, wide, 0)
    done = []
    for s in range(count):
        c = 8 * s
        spread = lambda x: jnp.broadcast_to(x, wide)
        lead = [spread(groups[s][i : i + 1, :]) for i in range(8)]
        pivot = {
            (i, j): spread(lead[i][:, c + j : c + j + 1]) for i in range(8) for j in range(i, 8)
        }
        below = range(s + 1, count)
        column = {t: [spread(groups[t][:, c + j : c + j + 1]) for j in range(8)] for t in below}
        keep = jnp.zeros(wide, F32)
        for j in range(8):
            r = lax.rsqrt(pivot[j, j])
            unit = lead[j] * r
            mult = {i: pivot[j, i] * r for i in range(j + 1, 8)}
            for i in range(j + 1, 8):
                for q in range(i, 8):
                    pivot[i, q] = pivot[i, q] - mult[i] * mult[q]
                lead[i] = lead[i] - mult[i] * unit
            for t in below:
                m = column[t][j] * r
                for i in range(j + 1, 8):
                    column[t][i] = column[t][i] - m * mult[i]
                groups[t] = groups[t] - m * unit
            keep = jnp.where(sub == j, unit, keep)
        done.append(keep)
    both = jnp.concatenate(done, axis=0)
    upper = jnp.where(rows <= cols, both[:, :half], 0.0)
    inverse = jnp.where(rows >= cols, both[:, half:], 0.0)
    return upper.T, inverse


def square(a, b, c):
    return jnp.concatenate(
        [
            jnp.concatenate([a, jnp.zeros_like(a)], axis=1),
            jnp.concatenate([b, c], axis=1),
        ],
        axis=0,
    )


def factor_in_place(a, w):
    n = a.shape[0]
    count = n // BLOCK

    def step(k, carry):
        o = pl.multiple_of(k * BLOCK, BLOCK)
        d = a[pl.ds(o, BLOCK), pl.ds(o, BLOCK)]
        l1, w1 = factor_half(d[:HALF, :HALF])
        l21 = full_dot(d[HALF:, :HALF], w1, NT)
        l2, w2 = factor_half(d[HALF:, HALF:] - full_dot(l21, l21, NT))
        w21 = -full_dot(w2, full_dot(l21, w1, NN), NN)
        a[pl.ds(o, BLOCK), pl.ds(o, BLOCK)] = square(l1, l21, l2)
        w[k] = square(w1, w21, w2)
        for at in range(count - 1):

            @pl.when(k == at)
            def _(at=at):
                low, high = at * BLOCK, at * BLOCK + BLOCK
                a[low:high, high:] = jnp.zeros((BLOCK, n - high), F32)
                p = full_dot(a[high:, low:high], w[at], NT)
                a[high:, low:high] = p
                for c in range(high, n, 2 * BLOCK):
                    e = min(c + 2 * BLOCK, n)
                    a[c:, c:e] = a[c:, c:e] - full_dot(p[c - high :], p[c - high : e - high], NT)

        return carry

    lax.fori_loop(0, count, step, 0)


def factor_kernel(x_ref, l_ref, w_ref):
    l_ref[...] = x_ref[...]
    factor_in_place(l_ref, w_ref)


def factor_call(whole):
    n = whole.shape[0]
    return pl.pallas_call(
        factor_kernel,
        name="factor",
        out_shape=(
            jax.ShapeDtypeStruct((n, n), F32),
            jax.ShapeDtypeStruct((n // BLOCK, BLOCK, BLOCK), F32),
        ),
        in_specs=[VMEM],
        out_specs=(VMEM, VMEM),
        compiler_params=pltpu.CompilerParams(vmem_limit_bytes=40 << 20),
        cost_estimate=pl.CostEstimate(flops=n**3 * 20, bytes_accessed=8 * n * n, transcendentals=0),
    )(whole)


def update_kernel(
    owners, slots, quarter, map_ref, l_ref, w_ref, br_ref, bc_ref, t_ref,
    panel_ref, out_ref, source_ref, xh, xl, lh, ll,
):
    n = l_ref.shape[0]
    q = br_ref.shape[0]
    share = panel_ref.shape[0]
    child = lax.axis_index("wide")
    row = lax.axis_index("grow")
    column = lax.axis_index("gcol")
    blocks = q // BLOCK
    per_owner = quarter // owners
    tile = 2 * BLOCK
    sides = (br_ref, bc_ref)
    lh[...], ll[...] = parts(l_ref[...])
    for k in range(n // BLOCK):
        low, high = k * BLOCK, k * BLOCK + BLOCK
        wk = parts(w_ref[k])

        def solve(i, carry, low=low, high=high, wk=wk):
            o = pl.multiple_of(i * tile, tile)
            for side, b in enumerate(sides):
                rest = b[pl.ds(o, tile), low:high]
                at = pl.ds(side * q + o, tile)
                if low:
                    rest = rest - split_dot(
                        (xh[at, :low], xl[at, :low]), (lh[low:high, :low], ll[low:high, :low]), NT
                    )
                x = split_dot(parts(rest), wk, NT)
                xh[at, low:high], xl[at, low:high] = parts(x)
                if side == 0:
                    br_ref[pl.ds(o, tile), low:high] = x
            return carry

        lax.fori_loop(0, q // tile, solve, 0)
    panel_ref[...] = br_ref[pl.ds(pl.multiple_of(column * share, share), share), :]

    def clear(i, carry):
        source_ref[i] = -1
        return carry

    lax.fori_loop(0, owners * per_owner, clear, 0)

    def place(g, carry):
        for b in range(blocks):
            to = map_ref[g, row * blocks + b] % quarter
            rank = jnp.int32(0)
            for e in range(b):
                other = map_ref[g, row * blocks + e] % quarter
                rank += (other // per_owner == to // per_owner).astype(jnp.int32)

            @pl.when(to // per_owner == child)
            def _(to=to, rank=rank):
                source_ref[g * per_owner + to % per_owner] = rank

        return carry

    lax.fori_loop(0, owners, place, 0)

    for b in range(blocks):
        o = b * BLOCK
        to = (map_ref[child, row * blocks + b] % quarter) // per_owner
        rank = jnp.int32(0)
        for e in range(b):
            other = (map_ref[child, row * blocks + e] % quarter) // per_owner
            rank += (other == to).astype(jnp.int32)
        out_ref[to * slots + rank] = t_ref[o : o + BLOCK, :] - split_dot(
            (xh[o : o + BLOCK, :], xl[o : o + BLOCK, :]), (xh[q:, :], xl[q:, :]), NT
        )


def update_call(row_map, factor, inverses, b_row, b_col, trailing, share, owners, slots, quarter):
    n = factor.shape[0]
    q = b_row.shape[0]
    return pl.pallas_call(
        functools.partial(update_kernel, owners, slots, quarter),
        name="update",
        out_shape=(
            jax.ShapeDtypeStruct((share, n), F32),
            jax.ShapeDtypeStruct((owners * slots, BLOCK, q), F32),
            jax.ShapeDtypeStruct((quarter,), jnp.int32),
        ),
        in_specs=[SMEM] + [VMEM] * 5,
        out_specs=(VMEM, VMEM, SMEM),
        scratch_shapes=[
            pltpu.VMEM((2 * q, n), BF16),
            pltpu.VMEM((2 * q, n), BF16),
            pltpu.VMEM((n, n), BF16),
            pltpu.VMEM((n, n), BF16),
        ],
        compiler_params=pltpu.CompilerParams(vmem_limit_bytes=56 << 20),
    )(row_map, factor, inverses, b_row, b_col, trailing)


def add_kernel(owners, map_ref, source_ref, parent_ref, in_ref, out_ref):
    p, g = pl.program_id(0), pl.program_id(1)
    per_owner = pl.num_programs(0)
    blocks = in_ref.shape[2] // BLOCK
    column_blocks = out_ref.shape[2] // BLOCK
    column = lax.axis_index("gcol")

    @pl.when(g == 0)
    def _():
        out_ref[...] = parent_ref[...]

    @pl.when(source_ref[g * per_owner + p] >= 0)
    def _():
        for b in range(blocks):
            to = map_ref[g, column * blocks + b] % column_blocks
            at = pl.ds(pl.multiple_of(to * BLOCK, BLOCK), BLOCK)
            out_ref[0, :, at] += in_ref[0, :, b * BLOCK : b * BLOCK + BLOCK]


def add_call(row_map, source, parent, incoming, owners, slots):
    _, rows, width = parent.shape
    per_owner = rows // BLOCK

    def pick(p, g, map_ref, source_ref):
        return (g * slots + jnp.maximum(source_ref[g * per_owner + p], 0), 0, 0)

    block = pl.BlockSpec((1, BLOCK, width), lambda p, g, *_: (0, p, 0))
    return pl.pallas_call(
        functools.partial(add_kernel, owners),
        name="extend_add",
        out_shape=jax.ShapeDtypeStruct(parent.shape, F32),
        grid_spec=pltpu.PrefetchScalarGridSpec(
            num_scalar_prefetch=2,
            grid=(per_owner, owners),
            in_specs=[block, pl.BlockSpec((1, BLOCK, incoming.shape[2]), pick)],
            out_specs=block,
        ),
        compiler_params=pltpu.CompilerParams(vmem_limit_bytes=32 << 20),
    )(row_map, source, parent, incoming)


def body(diag_block, lower_block, trailing_block, parent_front, row_map):
    owners = lax.axis_size("wide")
    rows, columns = lax.axis_size("grow"), lax.axis_size("gcol")
    share = diag_block.shape[1]
    row, column = lax.axis_index("grow"), lax.axis_index("gcol")
    whole = lax.all_gather(diag_block[0], ("grow", "gcol"), axis=0, tiled=True)
    b_row = lax.all_gather(lower_block[0], "gcol", axis=0, tiled=True)
    turn = [(a * columns + b, b * columns + a) for a in range(rows) for b in range(columns)]
    b_col = lax.ppermute(b_row, ("grow", "gcol"), turn)
    factor, inverses = factor_call(whole)
    factor_rows = lax.dynamic_slice_in_dim(factor, (row * columns + column) * share, share, 0)
    quarter = parent_front.shape[1] * owners // BLOCK
    blocks = trailing_block.shape[1] // BLOCK
    slots = min(blocks, quarter // owners)
    panel, outgoing, source = update_call(
        row_map, factor, inverses, b_row, b_col, trailing_block[0],
        lower_block.shape[1], owners, slots, quarter,
    )
    incoming = lax.all_to_all(outgoing, "wide", split_axis=0, concat_axis=0, tiled=True)
    parent = add_call(row_map, source, parent_front, incoming, owners, slots)
    return (factor_rows[None], panel[None], parent)


def solution(mesh):
    placed = (
        P("wide", ("grow", "gcol"), None),
        P("wide", ("grow", "gcol"), None),
        P("wide", "grow", "gcol"),
        P("grow", "wide", "gcol"),
        P(),
    )
    return jax.shard_map(
        body,
        mesh=mesh,
        in_specs=placed,
        out_specs=(
            P("wide", ("grow", "gcol"), None),
            P("wide", ("grow", "gcol"), None),
            P("grow", "wide", "gcol"),
        ),
        check_vma=False,
    )
```

time: 699 us -> 382 us (0.55); the launches traced: 688 us -> 381 us
  other arithmetic: 276 us -> 0 us
  Pallas kernels: 0 us -> 108 us
  matrix products: 67.8 us -> 0 us
  local copies, waits for them, and re-layouts: 69.7 us -> 11.7 us
  waiting for transfers between devices: 249 us -> 239 us
    another operation x33 -> x0, other arithmetic: 258 us -> none  [the longest x30 172 us: body(): factor = jnp.linalg.cholesky(whole)]
    pallas_call x0 -> x3, Pallas kernels: none -> 108 us  [the longest x1 49.5 us: factor_call(): pl.pallas_call(factor_kernel, name='factor', out_shape=(jax.ShapeDtypeStr...]
    all_gather x2 -> x1, waiting for transfers between devices: 144 us -> 67.1 us  [body(): b_row = lax.all_gather(lower_block[0], 'gcol', axis=0, tiled=True)]
    all_gather x1, waiting for transfers between devices: 54.6 us -> 119 us  [body(): whole = lax.all_gather(diag_block[0], ('grow', 'gcol'), axis=0, tiled=True)]
    another operation x29 -> x0, matrix products: 34.9 us -> none  [the longest x14 22.9 us: body(): factor = jnp.linalg.cholesky(whole)]
    another operation x34 -> x0, local copies, waits for them, and re-layouts: 34.9 us -> none
    dot_general x4 -> x0, matrix products: 32.9 us -> none  [the longest x1 10.5 us: body(): lax.dot_general(row_part, col_part, (((1,), (1,)), ((), ())), precision=h...]
    add x1 -> x0, other arithmetic: 11.9 us -> none  [body(): parent = parent_front + summed[None]]
  transfers between devices with their start and end apart: 4 -> 4, of which waited for: 4 -> 3; matrix products, arithmetic and copies ran while one was open for 0% -> 0% of each run, Pallas kernels for 0% -> 13%
where the time goes in v1:
time: 382 us; the launch traced here: 381 us
  waiting for transfers between devices  239 us (63%)
  Pallas kernels  108 us (28%)
  between operations  14.1 us (4%)
  local copies, waits for them, and re-layouts  11.7 us (3%)
  starting transfers between devices  8.41 us (2%)
    all_gather x1, waiting for transfers between devices, body(): whole = lax.all_gather(diag_block[0], ('grow', 'gcol'), axis=0, tiled=True)  119 us
    all_gather x1, waiting for transfers between devices, body(): b_row = lax.all_gather(lower_block[0], 'gcol', axis=0, tiled=True)  67.1 us
    all_to_all x1, waiting for transfers between devices, body(): lax.all_to_all(outgoing, 'wide', split_axis=0, concat_axis=0, tiled=True)  52 us
    pallas_call x1, Pallas kernels, factor_call(): pl.pallas_call(factor_kernel, name='factor', out_shape=(jax.ShapeDtypeStr...  49.5 us
    pallas_call x1, Pallas kernels, update_call(): pl.pallas_call(functools.partial(update_kernel, owners, slots, quarter),...  46.2 us
    pallas_call x1, Pallas kernels, add_call(): pl.pallas_call(functools.partial(add_kernel, owners), name='extend_add',...  12.1 us
    unnamed x14, local copies, waits for them, and re-layouts  10 us
  transfers between devices with their start and end apart: 4, of which 3 were waited for; matrix products, arithmetic and copies ran while one was open for 0% of the time, Pallas kernels for 13%

profile of v1, /device:TPU:0, one launch (start us, length us, event | category | flops | bytes accessed | tf_op | source)
XLA Modules:
  0.0 381.3 jit_solution(12382218545612797115)
XLA Ops:
  7.2 0.0 all-gather.7.cloned.1.call-start
  7.2 0.7 all-gather.7.cloned.1.call-update
  7.9 0.0 all-gather.5.cloned.1.call-start
  7.9 0.7 all-gather.5.cloned.1.call-update
  8.6 67.1 %all-gather.7.cloned.1.call-done = f32[1,768,1024]{2,1,0:T(8,128)} async-done(((f32[1,192,1024]{2,1,0:T(8,128)}), f32[1,768,1024]{2,1,0:T(8,128)}) %all-gather.7.cloned.1.call-update) | async-done | bytes 3145744 | tf_op jit(solution)/shard_map/all_gather | solution.py:280
  75.7 2.5 collective-permute-start
  78.3 118.8 %all-gather.5.cloned.1.call-done = f32[1,1024,1024]{2,1,0:T(8,128)} async-done(((f32[1,64,1024]{2,1,0:T(8,128)}), f32[1,1024,1024]{2,1,0:T(8,128)}) %all-gather.5.cloned.1.call-update) | async-done | bytes 4194320 | tf_op jit(solution)/shard_map/all_gather | solution.py:279
  197.1 2.2 copy-done.5
  199.2 49.5 %factor.1 = (f32[1024,1024]{1,0:T(8,128)S(1)}, f32[8,128,128]{2,1,0:T(8,128)S(1)}) custom-call(f32[1024,1024]{1,0:T(8,128)S(1)} %bitcast.6), custom_call_target="tpu_custom_call" | custom-call | flops 21474836480 | bytes 8388608 | tf_op jit(solution)/shard_map/factor/pallas_call | solution.py:125
  248.8 0.0 copy-start.1
  248.8 2.0 copy-done.1
  250.8 0.8 copy-done.2
  251.6 0.0 collective-permute-done.bc_ref
  251.6 1.6 copy-done.6
  253.3 46.2 %update.1 = (f32[192,1024]{1,0:T(8,128)}, f32[12,128,768]{2,1,0:T(8,128)}, s32[16]{0:T(128)}) custom-call(s32[2,24]{1,0:T(2,128)} %map_ref.3, f32[1024,1024]{1,0:T(8,128)} %copy-done.1, f32[8,128,128]{2,1,0:T(8,128)} %copy-done.2, f32[768,1024]{1,0:T(8,128)} %bitcast.8, f32[768,1024]{1,0:T(8,128)} %copy-done.6, f32[768,768]{1,0:T(8,128)} %bitcast.9), custom_call_target="tpu_custom_call" | custom-call | tf_op jit(solution)/shard_map/update/pallas_call | solution.py:213
  299.5 0.0 copy-start.3
  299.5 0.0 copy-start.4
  299.5 5.8 %all-to-all-start = ((f32[12,128,768]{2,1,0:T(8,128)}), f32[12,128,768]{2,1,0:T(8,128)}, u32[]{:S(2)}, u32[]{:S(2)}) async-start(f32[12,128,768]{2,1,0:T(8,128)} %get-tuple-element.12), calls=%async_computation | async-start | bytes 9437184 | tf_op jit(solution)/shard_map/all_to_all | solution.py:292
  305.3 1.7 dynamic-slice_bitcast_fusion
  307.0 52.0 %all-to-all-done.in_ref = f32[12,128,768]{2,1,0:T(8,128)} async-done(((f32[12,128,768]{2,1,0:T(8,128)}), f32[12,128,768]{2,1,0:T(8,128)}, u32[]{:S(2)}, u32[]{:S(2)}) %all-to-all-start) | async-done | bytes 4718624 | tf_op jit(solution)/shard_map/all_to_all | solution.py:292
  359.0 0.0 copy-done.3
  359.0 0.0 copy-done.4
  359.0 3.4 copy-done
  362.4 12.1 %extend_add.1 = f32[1,1024,2048]{2,1,0:T(8,128)} custom-call(s32[2,24]{1,0:T(2,128)S(1)} %copy-done.3, s32[16]{0:T(128)S(1)} %copy-done.4, f32[1,1024,2048]{2,1,0:T(8,128)S(1)} %copy-done, f32[12,128,768]{2,1,0:T(8,128)} %all-to-all-done.in_ref), custom_call_target="tpu_custom_call" | custom-call | tf_op jit(solution)/shard_map/extend_add/pallas_call | solution.py:260
  (4 shorter events, 0.0 us)
Async XLA Ops:
  7.2 68.6 %all-gather.7.cloned.1.call-start = ((), (), s32[]{:S(2)}) async-start(), calls=%async_computation.2 | async-start | bytes 3932160 | tf_op jit(solution)/shard_map/all_gather | solution.py:280
  7.9 189.2 %all-gather.5.cloned.1.call-start = ((), (), s32[]{:S(2)}) async-start(), calls=%async_computation.1 | async-start | bytes 4456448 | tf_op jit(solution)/shard_map/all_gather | solution.py:279
  75.7 175.9 %collective-permute-start = (f32[768,1024]{1,0:T(8,128)}, f32[768,1024]{1,0:T(8,128)S(1)}, u32[]{:S(2)}, u32[]{:S(2)}) collective-permute-start(f32[768,1024]{1,0:T(8,128)} %bitcast.7), channel_id=1, source_target_pairs={{0,0},{1,4},{2,8},{3,12},{4,1},{5,5},{6,9},{7,13},{8,2},{9,6},{10,... | collective-permute-start | bytes 9437192 | tf_op jit(solution)/shard_map/ppermute | solution.py:282
  197.1 2.2 copy-start.5
  248.8 2.0 copy-start.1
  250.8 0.8 copy-start.2
  251.6 1.7 copy-start.6
  299.5 59.5 %copy-start.3 = (s32[2,24]{1,0:T(2,128)S(1)}, s32[2,24]{1,0:T(2,128)}, u32[]{:S(2)}) copy-start(s32[2,24]{1,0:T(2,128)} %map_ref.3) | copy-start | bytes 580
  299.5 59.5 %copy-start.4 = (s32[16]{0:T(128)S(1)}, s32[16]{0:T(128)}, u32[]{:S(2)}) copy-start(s32[16]{0:T(128)} %get-tuple-element.11.source_ref) | copy-start | bytes 196
  299.5 59.5 %all-to-all-start = ((f32[12,128,768]{2,1,0:T(8,128)}), f32[12,128,768]{2,1,0:T(8,128)}, u32[]{:S(2)}, u32[]{:S(2)}) async-start(f32[12,128,768]{2,1,0:T(8,128)} %get-tuple-element.12), calls=%async_computation | async-start | bytes 9437184 | tf_op jit(solution)/shard_map/all_to_all | solution.py:292
  359.0 3.4 copy-start
Sparse Core Ops, SparseCore 0:
  9.5 66.1 all-gather.6
  77.9 119.0 all-gather.4

commit v2 on v1

--- a/solution.py
+++ b/solution.py
@@ -85,7 +85,7 @@
     )
 
 
-def factor_in_place(a, w):
+def factor_in_place(a, w, between):
     n = a.shape[0]
     count = n // BLOCK
 
@@ -109,31 +109,186 @@
                 for c in range(high, n, 2 * BLOCK):
                     e = min(c + 2 * BLOCK, n)
                     a[c:, c:e] = a[c:, c:e] - full_dot(p[c - high :], p[c - high : e - high], NT)
+                for act in between.get(at, ()):
+                    act()
 
         return carry
 
     lax.fori_loop(0, count, step, 0)
 
 
-def factor_kernel(x_ref, l_ref, w_ref):
-    l_ref[...] = x_ref[...]
-    factor_in_place(l_ref, w_ref)
-
-
-def factor_call(whole):
-    n = whole.shape[0]
+def gather_factor_kernel(
+    rows, columns, d_ref, x_ref, a, w, br, bc,
+    local, line_send, line_recv, far_send, far_recv, near_send, near_recv,
+    b_send, b_recv, c_send, c_recv,
+):
+    row, column = lax.axis_index("grow"), lax.axis_index("gcol")
+    far_row = lax.rem(row + rows // 2, rows)
+    near_row = row + 1 - 2 * lax.rem(row, 2)
+    right, left = {"gcol": column + 1}, {"gcol": column - 1}
+    far, near = {"grow": far_row}, {"grow": near_row}
+    share, part = d_ref.shape[0], x_ref.shape[0]
+    has_left, has_right = column > 0, column < columns - 1
+
+    def band(r, c):
+        return a.at[pl.ds(pl.multiple_of((r * columns + c) * share, share), share)]
+
+    def piece(ref, c):
+        return ref.at[pl.ds(pl.multiple_of(c * part, part), part)]
+
+    def remote(ref, send, recv, to):
+        return pltpu.make_async_remote_copy(
+            src_ref=ref, dst_ref=ref, send_sem=send, recv_sem=recv,
+            device_id=to, device_id_type=pl.DeviceIdType.MESH,
+        )
+
+    own_d = pltpu.make_async_copy(d_ref, band(row, column), local.at[0])
+    own_x = pltpu.make_async_copy(x_ref, piece(br, column), local.at[1])
+    own_d.start()
+    own_x.start()
+    barrier = pltpu.get_barrier_semaphore()
+    next_column = {"gcol": lax.rem(column + 1, columns)}
+    last_column = {"gcol": lax.rem(column + columns - 1, columns)}
+    for to in (far, near, next_column, last_column):
+        pl.semaphore_signal(barrier, inc=1, device_id=to, device_id_type=pl.DeviceIdType.MESH)
+    pl.semaphore_wait(barrier, 4)
+    own_d.wait()
+    own_x.wait()
+
+    def pass_on(ref, send, recv, c, both=False):
+        @pl.when((c <= column) & has_right)
+        def _():
+            remote(ref, send.at[0, c], recv.at[c], right).start()
+
+        @pl.when((c >= column) & has_left)
+        def _():
+            remote(ref, send.at[1, c], recv.at[c], left).start()
+
+    def passed(ref, send, recv, c):
+        @pl.when((c <= column) & has_right)
+        def _():
+            remote(ref, send.at[0, c], recv.at[c], right).wait_send()
+
+        @pl.when((c >= column) & has_left)
+        def _():
+            remote(ref, send.at[1, c], recv.at[c], left).wait_send()
+
+    def at_distance(d, act):
+        for c, there in ((column - d, column - d >= 0), (column + d, column + d < columns)):
+            pl.when(there)(functools.partial(act, c))
+
+    def spread(c):
+        remote(band(row, c), far_send.at[c], far_recv.at[c], far).start()
+        remote(band(row, c), near_send.at[0, c], near_recv.at[0, c], near).start()
+
+    pass_on(band(row, column), line_send, line_recv, column)
+    spread(column)
+
+    def arrived(c):
+        remote(band(row, c), line_send.at[0, c], line_recv.at[c], right).wait_recv()
+        pass_on(band(row, c), line_send, line_recv, c)
+        spread(c)
+
+    def crossed(c):
+        remote(band(far_row, c), far_send.at[c], far_recv.at[c], far).wait_recv()
+        remote(band(far_row, c), near_send.at[1, c], near_recv.at[1, c], near).start()
+
+    at_distance(1, arrived)
+    crossed(column)
+    for d in range(2, columns):
+        at_distance(d, arrived)
+        at_distance(d - 1, crossed)
+    pass_on(piece(br, column), b_send, b_recv, column)
+    at_distance(columns - 1, crossed)
+    near_far_row = lax.rem(near_row + rows // 2, rows)
+    for c in range(columns):
+        remote(band(near_row, c), near_send.at[0, c], near_recv.at[0, c], near).wait_recv()
+        remote(band(near_far_row, c), near_send.at[1, c], near_recv.at[1, c], near).wait_recv()
+    for c in range(columns):
+        remote(band(row, c), far_send.at[c], far_recv.at[c], far).wait_send()
+        remote(band(row, c), near_send.at[0, c], near_recv.at[0, c], near).wait_send()
+        remote(band(far_row, c), near_send.at[1, c], near_recv.at[1, c], near).wait_send()
+        passed(band(row, c), line_send, line_recv, c)
+
+    root = row == column
+    relay = far_row == column
+    from_far = relay
+    from_near = jnp.logical_not(root | relay)
+
+    def give(c):
+        @pl.when(root)
+        def _():
+            for slot, to in ((0, far), (1, near)):
+                pltpu.make_async_remote_copy(
+                    src_ref=piece(br, c), dst_ref=piece(bc, c), send_sem=c_send.at[slot, c],
+                    recv_sem=c_recv.at[c], device_id=to, device_id_type=pl.DeviceIdType.MESH,
+                ).start()
+
+    def take(c):
+        remote(piece(br, c), b_send.at[0, c], b_recv.at[c], right).wait_recv()
+        pass_on(piece(br, c), b_send, b_recv, c)
+        give(c)
+
+    def forward(c):
+        @pl.when(relay)
+        def _():
+            remote(piece(bc, c), c_send.at[0, c], c_recv.at[c], far).wait_recv()
+            remote(piece(bc, c), c_send.at[1, c], c_recv.at[c], near).start()
+
+    give(column)
+    between = {}
+    between[1] = [functools.partial(at_distance, 1, take)]
+    between[2] = [functools.partial(forward, column)]
+    between[3] = [functools.partial(at_distance, 2, take)]
+    between[4] = [functools.partial(at_distance, 1, forward)]
+    between[5] = [functools.partial(at_distance, d, take) for d in range(3, columns)]
+    between[6] = [functools.partial(at_distance, d, forward) for d in range(2, columns)]
+    factor_in_place(a, w, between)
+    for c in range(columns):
+        @pl.when(from_near)
+        def _(c=c):
+            remote(piece(bc, c), c_send.at[0, c], c_recv.at[c], near).wait_recv()
+
+        @pl.when(relay)
+        def _(c=c):
+            remote(piece(bc, c), c_send.at[1, c], c_recv.at[c], near).wait_send()
+
+        @pl.when(root)
+        def _(c=c):
+            remote(piece(br, c), c_send.at[0, c], c_recv.at[c], far).wait_send()
+            remote(piece(br, c), c_send.at[1, c], c_recv.at[c], near).wait_send()
+
+        passed(piece(br, c), b_send, b_recv, c)
+
+    @pl.when(root)
+    def _():
+        bc[...] = br[...]
+
+
+def gather_factor_call(diag, lower, rows, columns):
+    n = diag.shape[1]
+    q = lower.shape[0] * columns
+    dma = pltpu.SemaphoreType.DMA
     return pl.pallas_call(
-        factor_kernel,
-        name="factor",
+        functools.partial(gather_factor_kernel, rows, columns),
+        name="gather_factor",
         out_shape=(
             jax.ShapeDtypeStruct((n, n), F32),
             jax.ShapeDtypeStruct((n // BLOCK, BLOCK, BLOCK), F32),
+            jax.ShapeDtypeStruct((q, n), F32),
+            jax.ShapeDtypeStruct((q, n), F32),
         ),
-        in_specs=[VMEM],
-        out_specs=(VMEM, VMEM),
-        compiler_params=pltpu.CompilerParams(vmem_limit_bytes=40 << 20),
-        cost_estimate=pl.CostEstimate(flops=n**3 * 20, bytes_accessed=8 * n * n, transcendentals=0),
-    )(whole)
+        in_specs=[pl.BlockSpec(memory_space=pl.ANY)] * 2,
+        out_specs=(VMEM,) * 4,
+        scratch_shapes=[
+            dma((2,)), dma((2, columns)), dma((columns,)), dma((columns,)), dma((columns,)),
+            dma((2, columns)), dma((2, columns)), dma((2, columns)), dma((columns,)),
+            dma((2, columns)), dma((columns,)),
+        ],
+        compiler_params=pltpu.CompilerParams(
+            vmem_limit_bytes=40 << 20, collective_id=0, has_side_effects=True
+        ),
+    )(diag, lower)
 
 
 def update_kernel(
@@ -276,11 +431,9 @@
     rows, columns = lax.axis_size("grow"), lax.axis_size("gcol")
     share = diag_block.shape[1]
     row, column = lax.axis_index("grow"), lax.axis_index("gcol")
-    whole = lax.all_gather(diag_block[0], ("grow", "gcol"), axis=0, tiled=True)
-    b_row = lax.all_gather(lower_block[0], "gcol", axis=0, tiled=True)
-    turn = [(a * columns + b, b * columns + a) for a in range(rows) for b in range(columns)]
-    b_col = lax.ppermute(b_row, ("grow", "gcol"), turn)
-    factor, inverses = factor_call(whole)
+    factor, inverses, b_row, b_col = gather_factor_call(
+        diag_block[0], lower_block[0], rows, columns
+    )
     factor_rows = lax.dynamic_slice_in_dim(factor, (row * columns + column) * share, share, 0)
     quarter = parent_front.shape[1] * owners // BLOCK
     blocks = trailing_block.shape[1] // BLOCK

time: 382 us -> 225 us (0.59)
  waiting for transfers between devices: 239 us -> 50.6 us
  Pallas kernels: 108 us -> 152 us
  between operations: 14.1 us -> 0.7 us
    all_gather x2 -> x0, waiting for transfers between devices: 186 us -> none  [the longest x1 119 us: body(): whole = lax.all_gather(diag_block[0], ('grow', 'gcol'), axis=0, tiled=True)]
    pallas_call x1, Pallas kernels: 49.5 us -> 93.5 us  [gather_factor_call(): pl.pallas_call(functools.partial(gather_factor_kernel, rows, columns), na...]
    unnamed x14 -> x18, local copies, waits for them, and re-layouts: 10 us -> 11.6 us
  transfers between devices with their start and end apart: 4 -> 1, of which waited for: 3 -> 1; matrix products, arithmetic and copies ran while one was open for 0% -> 1% of each run, Pallas kernels for 13% -> 0%
where the time goes in v2:
time: 225 us; the launch traced here: 222 us
  Pallas kernels  152 us (68%)
  waiting for transfers between devices  50.6 us (22%)
  local copies, waits for them, and re-layouts  13.3 us (6%)
  starting transfers between devices  5.81 us (3%)
    pallas_call x1, Pallas kernels, gather_factor_call(): pl.pallas_call(functools.partial(gather_factor_kernel, rows, columns), na...  93.5 us
    all_to_all x1, waiting for transfers between devices, body(): lax.all_to_all(outgoing, 'wide', split_axis=0, concat_axis=0, tiled=True)  50.6 us
    pallas_call x1, Pallas kernels, update_call(): pl.pallas_call(functools.partial(update_kernel, owners, slots, quarter),...  46 us
    pallas_call x1, Pallas kernels, add_call(): pl.pallas_call(functools.partial(add_kernel, owners), name='extend_add',...  12.1 us
    unnamed x18, local copies, waits for them, and re-layouts  11.6 us
    all_to_all x1, starting transfers between devices, body(): lax.all_to_all(outgoing, 'wide', split_axis=0, concat_axis=0, tiled=True)  5.81 us
  transfers between devices with their start and end apart: 1, of which 1 were waited for; matrix products, arithmetic and copies ran while one was open for 1% of the time, Pallas kernels for 0%

profile of v2, /device:TPU:0, one launch (start us, length us, event | category | flops | bytes accessed | tf_op | source)
XLA Modules:
  0.0 222.1 jit_solution(9679440681801250230)
XLA Ops:
  0.6 0.0 copy-start.4
  0.6 1.1 copy-done.4
  1.8 0.0 copy-start.6
  1.8 0.9 copy-done.6
  2.7 93.5 %gather_factor.1 = (f32[1024,1024]{1,0:T(8,128)S(1)}, f32[8,128,128]{2,1,0:T(8,128)S(1)}, f32[768,1024]{1,0:T(8,128)S(1)}, f32[768,1024]{1,0:T(8,128)S(1)}) custom-call(f32[64,1024]{1,0:T(8,128)S(1)} %bitcast.7, f32[192,1024]{1,0:T(8,128)S(1)} %bitcast.6), custom_call_target="tpu_custom_call" | custom-call | tf_op jit(solution)/shard_map/gather_factor/pallas_call | solution.py:272
  96.3 0.0 copy-start.1
  96.3 1.9 copy-done.1
  98.2 0.0 copy-start.2
  98.2 1.7 copy-done.2
  99.9 0.0 copy-start.3
  99.9 1.7 copy-done.3
  101.6 0.0 copy-start.5
  101.6 0.8 copy-done.5
  102.4 46.0 %update.1 = (f32[192,1024]{1,0:T(8,128)}, f32[12,128,768]{2,1,0:T(8,128)}, s32[16]{0:T(128)}) custom-call(s32[2,24]{1,0:T(2,128)} %map_ref.3, f32[1024,1024]{1,0:T(8,128)} %copy-done.1, f32[8,128,128]{2,1,0:T(8,128)} %copy-done.5, f32[768,1024]{1,0:T(8,128)} %copy-done.2, f32[768,1024]{1,0:T(8,128)} %copy-done.3, f32[768,768]{1,0:T(8,128)} %bitcast.8), custom_call_target="tpu_custom_call" | custom-call | tf_op jit(solution)/shard_map/update/pallas_call | solution.py:368
  148.4 0.0 copy-start.7
  148.5 0.0 copy-start.8
  148.5 5.8 %all-to-all-start = ((f32[12,128,768]{2,1,0:T(8,128)}), f32[12,128,768]{2,1,0:T(8,128)}, u32[]{:S(2)}, u32[]{:S(2)}) async-start(f32[12,128,768]{2,1,0:T(8,128)} %get-tuple-element.16), calls=%async_computation | async-start | bytes 9437184 | tf_op jit(solution)/shard_map/all_to_all | solution.py:445
  154.3 1.7 dynamic-slice_bitcast_fusion
  156.0 50.6 %all-to-all-done.in_ref = f32[12,128,768]{2,1,0:T(8,128)} async-done(((f32[12,128,768]{2,1,0:T(8,128)}), f32[12,128,768]{2,1,0:T(8,128)}, u32[]{:S(2)}, u32[]{:S(2)}) %all-to-all-start) | async-done | bytes 4718624 | tf_op jit(solution)/shard_map/all_to_all | solution.py:445
  206.5 0.0 copy-done.7
  206.5 0.0 copy-done.8
  206.5 0.0 copy-start
  206.5 3.4 %copy-done = f32[1,1024,2048]{2,1,0:T(8,128)S(1)} copy-done((f32[1,1024,2048]{2,1,0:T(8,128)S(1)}, f32[1,1024,2048]{2,1,0:T(8,128)}, u32[]{:S(2)}) %copy-start) | copy-done | bytes 8388632
  209.9 12.1 %extend_add.1 = f32[1,1024,2048]{2,1,0:T(8,128)} custom-call(s32[2,24]{1,0:T(2,128)S(1)} %copy-done.7, s32[16]{0:T(128)S(1)} %copy-done.8, f32[1,1024,2048]{2,1,0:T(8,128)S(1)} %copy-done, f32[12,128,768]{2,1,0:T(8,128)} %all-to-all-done.in_ref), custom_call_target="tpu_custom_call" | custom-call | tf_op jit(solution)/shard_map/extend_add/pallas_call | solution.py:415
Async XLA Ops:
  0.6 1.1 copy-start.4
  1.8 0.9 copy-start.6
  96.3 2.0 copy-start.1
  98.2 1.7 copy-start.2
  99.9 1.7 copy-start.3
  101.6 0.8 copy-start.5
  148.4 58.1 %copy-start.7 = (s32[2,24]{1,0:T(2,128)S(1)}, s32[2,24]{1,0:T(2,128)}, u32[]{:S(2)}) copy-start(s32[2,24]{1,0:T(2,128)} %map_ref.3) | copy-start | bytes 580
  148.5 58.1 %copy-start.8 = (s32[16]{0:T(128)S(1)}, s32[16]{0:T(128)}, u32[]{:S(2)}) copy-start(s32[16]{0:T(128)} %get-tuple-element.15.source_ref) | copy-start | bytes 196
  148.5 58.1 %all-to-all-start = ((f32[12,128,768]{2,1,0:T(8,128)}), f32[12,128,768]{2,1,0:T(8,128)}, u32[]{:S(2)}, u32[]{:S(2)}) async-start(f32[12,128,768]{2,1,0:T(8,128)} %get-tuple-element.16), calls=%async_computation | async-start | bytes 9437184 | tf_op jit(solution)/shard_map/all_to_all | solution.py:445
  206.5 3.4 %copy-start = (f32[1,1024,2048]{2,1,0:T(8,128)S(1)}, f32[1,1024,2048]{2,1,0:T(8,128)}, u32[]{:S(2)}) copy-start(f32[1,1024,2048]{2,1,0:T(8,128)} %parent_ref.1) | copy-start | bytes 25165828

commit v3 on v2

--- a/solution.py
+++ b/solution.py
@@ -306,9 +306,12 @@
     tile = 2 * BLOCK
     sides = (br_ref, bc_ref)
     lh[...], ll[...] = parts(l_ref[...])
-    for k in range(n // BLOCK):
-        low, high = k * BLOCK, k * BLOCK + BLOCK
-        wk = parts(w_ref[k])
+    pair = 2 * BLOCK
+    for k in range(n // pair):
+        low, high = k * pair, k * pair + pair
+        wa, wb = w_ref[2 * k], w_ref[2 * k + 1]
+        across = l_ref[low + BLOCK : high, low : low + BLOCK]
+        wk = parts(square(wa, -full_dot(wb, full_dot(across, wa, NN), NN), wb))
 
         def solve(i, carry, low=low, high=high, wk=wk):
             o = pl.multiple_of(i * tile, tile)
@@ -350,16 +353,20 @@
 
     lax.fori_loop(0, owners, place, 0)
 
-    for b in range(blocks):
-        o = b * BLOCK
-        to = (map_ref[child, row * blocks + b] % quarter) // per_owner
-        rank = jnp.int32(0)
-        for e in range(b):
-            other = (map_ref[child, row * blocks + e] % quarter) // per_owner
-            rank += (other == to).astype(jnp.int32)
-        out_ref[to * slots + rank] = t_ref[o : o + BLOCK, :] - split_dot(
-            (xh[o : o + BLOCK, :], xl[o : o + BLOCK, :]), (xh[q:, :], xl[q:, :]), NT
-        )
+    step = 3 if blocks % 3 == 0 else 1
+    for first in range(0, blocks, step):
+        low, high = first * BLOCK, (first + step) * BLOCK
+        update = split_dot((xh[low:high, :], xl[low:high, :]), (xh[q:, :], xl[q:, :]), NT)
+        for b in range(first, first + step):
+            o = b * BLOCK
+            to = (map_ref[child, row * blocks + b] % quarter) // per_owner
+            rank = jnp.int32(0)
+            for e in range(b):
+                other = (map_ref[child, row * blocks + e] % quarter) // per_owner
+                rank += (other == to).astype(jnp.int32)
+            out_ref[to * slots + rank] = (
+                t_ref[o : o + BLOCK, :] - update[o - low : o - low + BLOCK, :]
+            )
 
 
 def update_call(row_map, factor, inverses, b_row, b_col, trailing, share, owners, slots, quarter):

time: 225 us -> 209 us (0.929)
  Pallas kernels: 152 us -> 136 us
    pallas_call x1, Pallas kernels: 46 us -> 30 us  [update_call(): pl.pallas_call(functools.partial(update_kernel, owners, slots, quarter),...]
where the time goes in v3:
time: 209 us; the launch traced here: 206 us
  Pallas kernels  136 us (65%)
  waiting for transfers between devices  50.6 us (24%)
  local copies, waits for them, and re-layouts  13.3 us (6%)
  starting transfers between devices  5.81 us (3%)
    pallas_call x1, Pallas kernels, gather_factor_call(): pl.pallas_call(functools.partial(gather_factor_kernel, rows, columns), na...  93.5 us
    all_to_all x1, waiting for transfers between devices, body(): lax.all_to_all(outgoing, 'wide', split_axis=0, concat_axis=0, tiled=True)  50.6 us
    pallas_call x1, Pallas kernels, update_call(): pl.pallas_call(functools.partial(update_kernel, owners, slots, quarter),...  30 us
    pallas_call x1, Pallas kernels, add_call(): pl.pallas_call(functools.partial(add_kernel, owners), name='extend_add',...  12.2 us
    unnamed x18, local copies, waits for them, and re-layouts  11.6 us
    all_to_all x1, starting transfers between devices, body(): lax.all_to_all(outgoing, 'wide', split_axis=0, concat_axis=0, tiled=True)  5.81 us
  transfers between devices with their start and end apart: 1, of which 1 were waited for; matrix products, arithmetic and copies ran while one was open for 1% of the time, Pallas kernels for 0%

profile of v3, /device:TPU:0, one launch (start us, length us, event | category | flops | bytes accessed | tf_op | source)
XLA Modules:
  0.0 206.0 jit_solution(1960702490066942595)
XLA Ops:
  0.6 0.0 copy-start.4
  0.6 1.1 copy-done.4
  1.8 0.0 copy-start.6
  1.8 0.9 copy-done.6
  2.7 93.5 %gather_factor.1 = (f32[1024,1024]{1,0:T(8,128)S(1)}, f32[8,128,128]{2,1,0:T(8,128)S(1)}, f32[768,1024]{1,0:T(8,128)S(1)}, f32[768,1024]{1,0:T(8,128)S(1)}) custom-call(f32[64,1024]{1,0:T(8,128)S(1)} %bitcast.7, f32[192,1024]{1,0:T(8,128)S(1)} %bitcast.6), custom_call_target="tpu_custom_call" | custom-call | tf_op jit(solution)/shard_map/gather_factor/pallas_call | solution.py:272
  96.3 0.0 copy-start.1
  96.3 1.9 copy-done.1
  98.2 0.0 copy-start.2
  98.2 1.7 copy-done.2
  99.9 0.0 copy-start.3
  99.9 1.7 copy-done.3
  101.6 0.0 copy-start.5
  101.6 0.8 copy-done.5
  102.4 30.0 %update.1 = (f32[192,1024]{1,0:T(8,128)}, f32[12,128,768]{2,1,0:T(8,128)}, s32[16]{0:T(128)}) custom-call(s32[2,24]{1,0:T(2,128)} %map_ref.3, f32[1024,1024]{1,0:T(8,128)} %copy-done.1, f32[8,128,128]{2,1,0:T(8,128)} %copy-done.5, f32[768,1024]{1,0:T(8,128)} %copy-done.2, f32[768,1024]{1,0:T(8,128)} %copy-done.3, f32[768,768]{1,0:T(8,128)} %bitcast.8), custom_call_target="tpu_custom_call" | custom-call | tf_op jit(solution)/shard_map/update/pallas_call | solution.py:375
  132.4 0.0 copy-start.7
  132.4 0.0 copy-start.8
  132.4 5.8 %all-to-all-start = ((f32[12,128,768]{2,1,0:T(8,128)}), f32[12,128,768]{2,1,0:T(8,128)}, u32[]{:S(2)}, u32[]{:S(2)}) async-start(f32[12,128,768]{2,1,0:T(8,128)} %get-tuple-element.16), calls=%async_computation | async-start | bytes 9437184 | tf_op jit(solution)/shard_map/all_to_all | solution.py:452
  138.3 1.7 dynamic-slice_bitcast_fusion
  139.9 50.6 %all-to-all-done.in_ref = f32[12,128,768]{2,1,0:T(8,128)} async-done(((f32[12,128,768]{2,1,0:T(8,128)}), f32[12,128,768]{2,1,0:T(8,128)}, u32[]{:S(2)}, u32[]{:S(2)}) %all-to-all-start) | async-done | bytes 4718624 | tf_op jit(solution)/shard_map/all_to_all | solution.py:452
  190.5 0.0 copy-done.7
  190.5 0.0 copy-done.8
  190.5 0.0 copy-start
  190.5 3.4 %copy-done = f32[1,1024,2048]{2,1,0:T(8,128)S(1)} copy-done((f32[1,1024,2048]{2,1,0:T(8,128)S(1)}, f32[1,1024,2048]{2,1,0:T(8,128)}, u32[]{:S(2)}) %copy-start) | copy-done | bytes 8388632
  193.9 12.2 %extend_add.1 = f32[1,1024,2048]{2,1,0:T(8,128)} custom-call(s32[2,24]{1,0:T(2,128)S(1)} %copy-done.7, s32[16]{0:T(128)S(1)} %copy-done.8, f32[1,1024,2048]{2,1,0:T(8,128)S(1)} %copy-done, f32[12,128,768]{2,1,0:T(8,128)} %all-to-all-done.in_ref), custom_call_target="tpu_custom_call" | custom-call | tf_op jit(solution)/shard_map/extend_add/pallas_call | solution.py:422
Async XLA Ops:
  0.6 1.1 copy-start.4
  1.8 0.9 copy-start.6
  96.3 2.0 copy-start.1
  98.2 1.7 copy-start.2
  99.9 1.7 copy-start.3
  101.6 0.8 copy-start.5
  132.4 58.1 %copy-start.7 = (s32[2,24]{1,0:T(2,128)S(1)}, s32[2,24]{1,0:T(2,128)}, u32[]{:S(2)}) copy-start(s32[2,24]{1,0:T(2,128)} %map_ref.3) | copy-start | bytes 580
  132.4 58.1 %copy-start.8 = (s32[16]{0:T(128)S(1)}, s32[16]{0:T(128)}, u32[]{:S(2)}) copy-start(s32[16]{0:T(128)} %get-tuple-element.15.source_ref) | copy-start | bytes 196
  132.4 58.1 %all-to-all-start = ((f32[12,128,768]{2,1,0:T(8,128)}), f32[12,128,768]{2,1,0:T(8,128)}, u32[]{:S(2)}, u32[]{:S(2)}) async-start(f32[12,128,768]{2,1,0:T(8,128)} %get-tuple-element.16), calls=%async_computation | async-start | bytes 9437184 | tf_op jit(solution)/shard_map/all_to_all | solution.py:452
  190.5 3.4 %copy-start = (f32[1,1024,2048]{2,1,0:T(8,128)S(1)}, f32[1,1024,2048]{2,1,0:T(8,128)}, u32[]{:S(2)}) copy-start(f32[1,1024,2048]{2,1,0:T(8,128)} %parent_ref.1) | copy-start | bytes 25165828
